TPU v7x, 32 devices: a whole 2x2x4 slice. The times are simulated.
32 devices in a mesh: dp: 4 (over x, core), ctx: 8 (over z, y).
Axes of the slice: x: 2, y: 2, z: 4, core: 2. Of those that a mesh axis runs over, the one named last changes fastest.
Arguments:
- queries: bfloat16 [16384, 32, 128], P(('dp', 'ctx')), may hold values from -8 to 8
- keys: bfloat16 [16384, 4, 128], P(('dp', 'ctx')), may hold values from -8 to 8
- values: bfloat16 [16384, 4, 128], P(('dp', 'ctx')), may hold values from -6 to 6
- doc_lengths: int32 [4, 8], P('dp'), may hold values from 1 to 1024, 4096 in all within a row
Outputs:
- attended: bfloat16 [16384, 32, 128], P(('dp', 'ctx'))
All inputs are finite; a program needn't handle non-finite values.
Results may differ from a plain program's by a relative error of at most 0.0035.
Values may be sent and summed in bfloat16 or wider, within the bound.
A program may use at most 128 MiB of HBM per device.

v0:
```python
import math

import jax
import jax.numpy as jnp
from jax import lax
from jax.sharding import PartitionSpec as P


def shifted(value, axis, steps):
    count = lax.axis_size(axis)
    first, last = (max(0, -steps), min(count, count - steps))
    return lax.ppermute(value, axis, [(source, source + steps) for source in range(first, last)])


def doc_index(positions, lengths):
    doc_ends = jnp.cumsum(lengths)
    return jnp.sum((positions[:, None] >= doc_ends[None, :]).astype(jnp.int32), axis=1)


def tile_partial(tile_queries, block_keys, block_values, query_pos, key_pos, lengths):
    tile_rows, head_count, head_width = tile_queries.shape
    kv_count = block_keys.shape[1]
    group_size = head_count // kv_count
    allowed = doc_index(query_pos, lengths)[:, None] == doc_index(key_pos, lengths)[None, :]
    allowed = allowed & (key_pos[None, :] <= query_pos[:, None]) & (key_pos[None, :] >= 0)
    score_scale = 1.0 / math.sqrt(head_width)
    grouped = tile_queries.reshape(tile_rows, kv_count, group_size, head_width).transpose(
        1, 0, 2, 3
    )
    key_heads = block_keys.transpose(1, 0, 2)
    value_heads = block_values.transpose(1, 0, 2)

    def one_head(operands):
        query_group, key_head, value_head = operands
        scores = (
            jnp.einsum("tgd,ud->gtu", query_group, key_head, preferred_element_type=jnp.float32)
            * score_scale
        )
        masked = jnp.where(allowed[None], scores, -1e30)
        maxima = jnp.max(masked, axis=-1)
        weights = jnp.where(allowed[None], jnp.exp(masked - maxima[..., None]), 0.0)
        sums = jnp.sum(weights, axis=-1)
        rounded = weights.astype(jnp.bfloat16)
        outputs = jnp.einsum("gtu,ud->tgd", rounded, value_head, preferred_element_type=jnp.float32)
        return (maxima, sums, outputs)

    maxima, sums, outputs = lax.map(one_head, (grouped, key_heads, value_heads))
    maxima = maxima.reshape(head_count, tile_rows)
    sums = sums.reshape(head_count, tile_rows)
    outputs = outputs.transpose(1, 0, 2, 3).reshape(tile_rows, head_count, head_width)
    return (maxima, sums, outputs)


def merge_tiles(partials):
    row_max = partials[0][0]
    for part_item in partials[1:]:
        row_max = jnp.maximum(row_max, part_item[0])
    denominator = 0.0
    weighted = 0.0
    for maxima, sums, outputs in partials:
        factor = jnp.exp(maxima - row_max)
        denominator = denominator + factor * sums
        weighted = weighted + factor.T[:, :, None] * outputs
    return (weighted / denominator.T[:, :, None]).astype(jnp.bfloat16)


def body(queries, keys, values, doc_lengths):
    tile_rows, head_count, head_width = queries.shape
    shard_index = lax.axis_index("ctx")
    lengths_row = doc_lengths[0]
    query_pos = shard_index * tile_rows + jnp.arange(tile_rows, dtype=jnp.int32)
    key_value = jnp.stack([keys, values])
    near_pair = shifted(key_value, "ctx", 1)
    far_pair = shifted(key_value, "ctx", 2)
    first_pos = shard_index * tile_rows
    doc_ids = doc_index(
        jnp.stack([first_pos, first_pos - 1, first_pos - tile_rows - 1]), lengths_row
    )
    reach_near = (shard_index >= 1) & (doc_ids[0] == doc_ids[1])
    reach_far = (shard_index >= 2) & (doc_ids[0] == doc_ids[2])
    nothing = (
        jnp.full((head_count, tile_rows), -1e30, jnp.float32),
        jnp.zeros((head_count, tile_rows), jnp.float32),
        jnp.zeros((tile_rows, head_count, head_width), jnp.float32),
    )

    def maybe_tile(flag, tile_queries, key_pair, offset, lengths):

        def compute():
            return tile_partial(
                tile_queries,
                key_pair[0],
                key_pair[1],
                query_pos,
                query_pos - offset * tile_rows,
                lengths,
            )

        def skipped():
            return nothing

        return lax.cond(flag, compute, skipped)

    diagonal = tile_partial(queries, keys, values, query_pos, query_pos, lengths_row)
    nearby = maybe_tile(reach_near, queries, near_pair, 1, lengths_row)
    distant = maybe_tile(reach_far, queries, far_pair, 2, lengths_row)
    return merge_tiles([diagonal, nearby, distant])


def solution(mesh):
    placed = (
        P(("dp", "ctx"), None, None),
        P(("dp", "ctx"), None, None),
        P(("dp", "ctx"), None, None),
        P("dp", None),
    )
    return jax.shard_map(
        body, mesh=mesh, in_specs=placed, out_specs=P(("dp", "ctx"), None, None), check_vma=False
    )
```

profile of v0, /device:TPU:8, one launch (start us, length us, event | category | flops | bytes accessed | tf_op | source)
XLA Modules:
  0.0 195.2 jit_solution(15899072904548712695)
XLA Ops:
  11.9 5.8 %copy.30 = bf16[512,32,128]{2,0,1:T(8,128)(2,1)} copy(bf16[512,32,128]{2,1,0:T(8,128)(2,1)} %param.14) | data formatting | bytes 8388608 | tf_op args[0]
  18.0 35.8 %while.45 = (s32[]{:T(128)}, f32[4,8,512]{2,1,0:T(8,128)S(1)}, f32[4,8,512]{2,1,0:T(8,128)S(1)}, f32[4,512,8,128]{1,3,2,0:T(8,128)}, bf16[4,512,128]{2,1,0:T(8,1...) while((s32[]{:T(128)}, f32[4,8,512]{2,1,0:T(8,128)S(1)}, ...), condition=%wide.region_5.6_spmd.clone, body=%wide.region_2.0_spmd.clone.sunk | while | flops 1102045184 | bytes 29760112 | solution.py:47
  21.0 3.9 %bitcast_dynamic-update-slice_fusion.16 = f32[4,512,8,128]{1,3,2,0:T(8,128)} fusion(f32[4,512,8,128]{1,3,2,0:T(8,128)} %get-tuple-element.707, s32[]{:T(128)} %get-tuple-element.704, f32[512,512,8]{1,0,2:T(8,128)S(1)} %get-tuple-element.567, f32[8,512]{1,0:T(8,128)S(1)} %get-tuple-element.568, pred[512,512]{0,1:T(8,128)(4,1)S(1)} %and_and_fusion.6, ...), kind=kOutput, calls=%fused_computation.68.clone.1 | convolution fusion | flops 547356672 | bytes 10896384 | tf_op jit(solution)/shard_map/while/body/eval_jaxpr/gtu,ud->tgd/dot_general | solution.py:44
  30.0 3.8 %bitcast_dynamic-update-slice_fusion.16 = f32[4,512,8,128]{1,3,2,0:T(8,128)} fusion(f32[4,512,8,128]{1,3,2,0:T(8,128)} %get-tuple-element.707, s32[]{:T(128)} %get-tuple-element.704, f32[512,512,8]{1,0,2:T(8,128)S(1)} %get-tuple-element.567, f32[8,512]{1,0:T(8,128)S(1)} %get-tuple-element.568, pred[512,512]{0,1:T(8,128)(4,1)S(1)} %and_and_fusion.6, ...), kind=kOutput, calls=%fused_computation.68.clone.1 | convolution fusion | flops 547356672 | bytes 10896384 | tf_op jit(solution)/shard_map/while/body/eval_jaxpr/gtu,ud->tgd/dot_general | solution.py:44
  38.9 3.9 %bitcast_dynamic-update-slice_fusion.16 = f32[4,512,8,128]{1,3,2,0:T(8,128)} fusion(f32[4,512,8,128]{1,3,2,0:T(8,128)} %get-tuple-element.707, s32[]{:T(128)} %get-tuple-element.704, f32[512,512,8]{1,0,2:T(8,128)S(1)} %get-tuple-element.567, f32[8,512]{1,0:T(8,128)S(1)} %get-tuple-element.568, pred[512,512]{0,1:T(8,128)(4,1)S(1)} %and_and_fusion.6, ...), kind=kOutput, calls=%fused_computation.68.clone.1 | convolution fusion | flops 547356672 | bytes 10896384 | tf_op jit(solution)/shard_map/while/body/eval_jaxpr/gtu,ud->tgd/dot_general | solution.py:44
  47.9 3.8 %bitcast_dynamic-update-slice_fusion.16 = f32[4,512,8,128]{1,3,2,0:T(8,128)} fusion(f32[4,512,8,128]{1,3,2,0:T(8,128)} %get-tuple-element.707, s32[]{:T(128)} %get-tuple-element.704, f32[512,512,8]{1,0,2:T(8,128)S(1)} %get-tuple-element.567, f32[8,512]{1,0:T(8,128)S(1)} %get-tuple-element.568, pred[512,512]{0,1:T(8,128)(4,1)S(1)} %and_and_fusion.6, ...), kind=kOutput, calls=%fused_computation.68.clone.1 | convolution fusion | flops 547356672 | bytes 10896384 | tf_op jit(solution)/shard_map/while/body/eval_jaxpr/gtu,ud->tgd/dot_general | solution.py:44
  57.3 10.3 %copy.37 = f32[512,4,8,128]{3,2,1,0:T(8,128)} copy(f32[512,4,8,128]{0,3,2,1:T(8,128)} %bitcast.258) | data formatting | bytes 16777216 | tf_op jit(solution)/shard_map/transpose | solution.py:50
  67.6 57.0 %conditional.2 = (f32[32,512]{1,0:T(8,128)}, f32[32,512]{1,0:T(8,128)}, f32[512,32,128]{2,1,0:T(8,128)}) conditional(s32[]{:T(128)} %convert_element_type.39, () %tuple.34, (bf16[512,32,128]{2,1,0:T(8,128)(2,1)}, bf16[2,512,4,128]{1,3,2,0:T(8,128)(2,1)S(1)}, s32[512]{0:T(512)S(1)}, s32[8]{0:T(128)S(1)}) %tuple.124), branch_computations={%region_7.8_spmd, %region_8.0_spmd} | conditional | flops 1102070272 | bytes 59139944 | solution.py:102
  70.4 5.8 %copy.34 = bf16[512,32,128]{2,0,1:T(8,128)(2,1)} copy(bf16[512,32,128]{2,1,0:T(8,128)(2,1)} %get-tuple-element.271) | data formatting | bytes 8388608 | tf_op jit(solution)/shard_map
  76.2 38.1 %while.43 = (s32[]{:T(128)}, f32[4,8,512]{2,1,0:T(8,128)}, f32[4,8,512]{2,1,0:T(8,128)}, f32[4,512,8,128]{1,3,2,0:T(8,128)}, bf16[4,512,128]{2,1,0:T(8,128)(2,1)...) while((s32[]{:T(128)}, f32[4,8,512]{2,1,0:T(8,128)}, ...), condition=%wide.region_15.15_spmd.clone, body=%wide.region_12.14_spmd.clone.sunk | while | flops 1102045184 | bytes 29764732 | solution.py:47
  79.2 3.9 %bitcast_dynamic-update-slice_fusion.20 = f32[4,512,8,128]{1,3,2,0:T(8,128)} fusion(f32[4,512,8,128]{1,3,2,0:T(8,128)} %get-tuple-element.658, s32[]{:T(128)} %get-tuple-element.655, f32[512,512,8]{1,0,2:T(8,128)S(1)} %get-tuple-element.599, f32[8,512]{1,0:T(8,128)S(1)} %get-tuple-element.600, pred[512,512]{0,1:T(8,128)(4,1)S(1)} %and_and_fusion.8, ...), kind=kOutput, calls=%fused_computation.10.clone.1 | convolution fusion | flops 547356672 | bytes 10896384 | tf_op jit(solution)/shard_map/cond/branch_1_fun/while/body/eval_jaxpr/gtu,ud->tgd/dot_general | solution.py:44
  88.8 3.8 %bitcast_dynamic-update-slice_fusion.20 = f32[4,512,8,128]{1,3,2,0:T(8,128)} fusion(f32[4,512,8,128]{1,3,2,0:T(8,128)} %get-tuple-element.658, s32[]{:T(128)} %get-tuple-element.655, f32[512,512,8]{1,0,2:T(8,128)S(1)} %get-tuple-element.599, f32[8,512]{1,0:T(8,128)S(1)} %get-tuple-element.600, pred[512,512]{0,1:T(8,128)(4,1)S(1)} %and_and_fusion.8, ...), kind=kOutput, calls=%fused_computation.10.clone.1 | convolution fusion | flops 547356672 | bytes 10896384 | tf_op jit(solution)/shard_map/cond/branch_1_fun/while/body/eval_jaxpr/gtu,ud->tgd/dot_general | solution.py:44
  98.3 3.9 %bitcast_dynamic-update-slice_fusion.20 = f32[4,512,8,128]{1,3,2,0:T(8,128)} fusion(f32[4,512,8,128]{1,3,2,0:T(8,128)} %get-tuple-element.658, s32[]{:T(128)} %get-tuple-element.655, f32[512,512,8]{1,0,2:T(8,128)S(1)} %get-tuple-element.599, f32[8,512]{1,0:T(8,128)S(1)} %get-tuple-element.600, pred[512,512]{0,1:T(8,128)(4,1)S(1)} %and_and_fusion.8, ...), kind=kOutput, calls=%fused_computation.10.clone.1 | convolution fusion | flops 547356672 | bytes 10896384 | tf_op jit(solution)/shard_map/cond/branch_1_fun/while/body/eval_jaxpr/gtu,ud->tgd/dot_general | solution.py:44
  107.8 3.8 %bitcast_dynamic-update-slice_fusion.20 = f32[4,512,8,128]{1,3,2,0:T(8,128)} fusion(f32[4,512,8,128]{1,3,2,0:T(8,128)} %get-tuple-element.658, s32[]{:T(128)} %get-tuple-element.655, f32[512,512,8]{1,0,2:T(8,128)S(1)} %get-tuple-element.599, f32[8,512]{1,0:T(8,128)S(1)} %get-tuple-element.600, pred[512,512]{0,1:T(8,128)(4,1)S(1)} %and_and_fusion.8, ...), kind=kOutput, calls=%fused_computation.10.clone.1 | convolution fusion | flops 547356672 | bytes 10896384 | tf_op jit(solution)/shard_map/cond/branch_1_fun/while/body/eval_jaxpr/gtu,ud->tgd/dot_general | solution.py:44
  114.3 10.3 %copy.47 = f32[512,32,128]{2,1,0:T(8,128)} copy(f32[512,32,128]{0,2,1:T(8,128)} %bitcast.259) | data formatting | bytes 16777216 | tf_op jit(solution)/shard_map/cond | solution.py:102
  124.6 55.3 %conditional.3 = (f32[32,512]{1,0:T(8,128)}, f32[32,512]{1,0:T(8,128)}, f32[512,32,128]{2,1,0:T(8,128)}) conditional(s32[]{:T(128)} %convert_element_type.40, () %tuple.36, (bf16[512,32,128]{2,1,0:T(8,128)(2,1)}, bf16[2,512,4,128]{1,3,2,0:T(8,128)(2,1)S(1)}, s32[512]{0:T(512)S(1)}, s32[8]{0:T(128)S(1)}) %tuple.125), branch_computations={%region_16.17_spmd, %region_17.25_spmd} | conditional | flops 1102070272 | bytes 59139944 | solution.py:102
  125.6 5.8 %copy.35 = bf16[512,32,128]{2,0,1:T(8,128)(2,1)} copy(bf16[512,32,128]{2,1,0:T(8,128)(2,1)} %get-tuple-element.275) | data formatting | bytes 8388608 | tf_op jit(solution)/shard_map
  131.5 38.1 %while.44 = (s32[]{:T(128)}, f32[4,8,512]{2,1,0:T(8,128)}, f32[4,8,512]{2,1,0:T(8,128)}, f32[4,512,8,128]{1,3,2,0:T(8,128)}, bf16[4,512,128]{2,1,0:T(8,128)(2,1)...) while((s32[]{:T(128)}, f32[4,8,512]{2,1,0:T(8,128)}, ...), condition=%wide.region_24.24_spmd.clone, body=%wide.region_21.23_spmd.clone.sunk | while | flops 1102045184 | bytes 29764732 | solution.py:47
  134.5 3.9 %bitcast_dynamic-update-slice_fusion.18 = f32[4,512,8,128]{1,3,2,0:T(8,128)} fusion(f32[4,512,8,128]{1,3,2,0:T(8,128)} %get-tuple-element.619, s32[]{:T(128)} %get-tuple-element.616, f32[512,512,8]{1,0,2:T(8,128)S(1)} %get-tuple-element.583, f32[8,512]{1,0:T(8,128)S(1)} %get-tuple-element.584, pred[512,512]{0,1:T(8,128)(4,1)S(1)} %and_and_fusion.7, ...), kind=kOutput, calls=%fused_computation.39.clone.1 | convolution fusion | flops 547356672 | bytes 10896384 | tf_op jit(solution)/shard_map/cond/branch_1_fun/while/body/eval_jaxpr/gtu,ud->tgd/dot_general | solution.py:44
  144.1 3.8 %bitcast_dynamic-update-slice_fusion.18 = f32[4,512,8,128]{1,3,2,0:T(8,128)} fusion(f32[4,512,8,128]{1,3,2,0:T(8,128)} %get-tuple-element.619, s32[]{:T(128)} %get-tuple-element.616, f32[512,512,8]{1,0,2:T(8,128)S(1)} %get-tuple-element.583, f32[8,512]{1,0:T(8,128)S(1)} %get-tuple-element.584, pred[512,512]{0,1:T(8,128)(4,1)S(1)} %and_and_fusion.7, ...), kind=kOutput, calls=%fused_computation.39.clone.1 | convolution fusion | flops 547356672 | bytes 10896384 | tf_op jit(solution)/shard_map/cond/branch_1_fun/while/body/eval_jaxpr/gtu,ud->tgd/dot_general | solution.py:44
  153.6 3.9 %bitcast_dynamic-update-slice_fusion.18 = f32[4,512,8,128]{1,3,2,0:T(8,128)} fusion(f32[4,512,8,128]{1,3,2,0:T(8,128)} %get-tuple-element.619, s32[]{:T(128)} %get-tuple-element.616, f32[512,512,8]{1,0,2:T(8,128)S(1)} %get-tuple-element.583, f32[8,512]{1,0:T(8,128)S(1)} %get-tuple-element.584, pred[512,512]{0,1:T(8,128)(4,1)S(1)} %and_and_fusion.7, ...), kind=kOutput, calls=%fused_computation.39.clone.1 | convolution fusion | flops 547356672 | bytes 10896384 | tf_op jit(solution)/shard_map/cond/branch_1_fun/while/body/eval_jaxpr/gtu,ud->tgd/dot_general | solution.py:44
  163.1 3.8 %bitcast_dynamic-update-slice_fusion.18 = f32[4,512,8,128]{1,3,2,0:T(8,128)} fusion(f32[4,512,8,128]{1,3,2,0:T(8,128)} %get-tuple-element.619, s32[]{:T(128)} %get-tuple-element.616, f32[512,512,8]{1,0,2:T(8,128)S(1)} %get-tuple-element.583, f32[8,512]{1,0:T(8,128)S(1)} %get-tuple-element.584, pred[512,512]{0,1:T(8,128)(4,1)S(1)} %and_and_fusion.7, ...), kind=kOutput, calls=%fused_computation.39.clone.1 | convolution fusion | flops 547356672 | bytes 10896384 | tf_op jit(solution)/shard_map/cond/branch_1_fun/while/body/eval_jaxpr/gtu,ud->tgd/dot_general | solution.py:44
  169.6 10.3 %copy.49 = f32[512,32,128]{2,1,0:T(8,128)} copy(f32[512,32,128]{0,2,1:T(8,128)} %bitcast.260) | data formatting | bytes 16777216 | tf_op jit(solution)/shard_map/cond | solution.py:102
  181.4 13.7 %fusion.69 = bf16[512,32,128]{2,1,0:T(8,128)(2,1)} fusion(f32[512,32,128]{2,1,0:T(8,128)} %get-tuple-element.280, f32[512,32,128]{2,1,0:T(8,128)} %get-tuple-element.279, f32[512,4,8,128]{3,2,1,0:T(8,128)} %copy.37, f32[512,32]{1,0:T(8,128)S(1)} %copy.42, f32[512,32]{1,0:T(8,128)S(1)} %copy.40, f32[512,32]{1,0:T(8,128)S(1)} %copy.38, f32[512,32]{1,0:T(8,128)S(1)} %copy.36), kind=kLoop, calls=%fused_computation.88 | loop fusion | flops 14680064 | bytes 29622272 | tf_op jit(solution)/shard_map/convert_element_type | solution.py:64
  (93 shorter events, 83.7 us)
Async XLA Ops:
  0.0 17.7 %copy-start = (s32[1,8]{1,0:T(1,128)S(1)}, s32[1,8]{1,0:T(1,128)}, u32[]{:S(2)}) copy-start(s32[1,8]{1,0:T(1,128)} %param.17) | copy-start | bytes 100
  3.8 63.8 %collective-permute-start = (bf16[2,512,4,128]{1,3,2,0:T(8,128)(2,1)}, bf16[2,512,4,128]{1,3,2,0:T(8,128)(2,1)S(1)}, u32[]{:S(2)}, u32[]{:S(2)}) collective-permute-start(bf16[2,512,4,128]{1,3,2,0:T(8,128)(2,1)} %pad_maximum_fusion), channel_id=1, source_target_pairs={{0,1},{1,2},{2,3},{3,4},{4,5},{5,6},{6,7},{8,9},{9,10},{10,11},{11... | collective-permute-start | bytes 3145736 | tf_op jit(solution)/shard_map/ppermute | solution.py:12
  7.2 117.4 %collective-permute-start.1 = (bf16[2,512,4,128]{1,3,2,0:T(8,128)(2,1)}, bf16[2,512,4,128]{1,3,2,0:T(8,128)(2,1)S(1)}, u32[]{:S(2)}, u32[]{:S(2)}) collective-permute-start(bf16[2,512,4,128]{1,3,2,0:T(8,128)(2,1)} %pad_maximum_fusion), channel_id=1, source_target_pairs={{0,2},{1,3},{2,4},{3,5},{4,6},{5,7},{8,10},{9,11},{10,12},{11,13},... | collective-permute-start | bytes 3145736 | tf_op jit(solution)/shard_map/ppermute | solution.py:12
where the time goes:
time: 197 us; the launch traced here: 195 us
  matrix products  78.8 us (40%)
  local copies, waits for them, and re-layouts  61.4 us (31%)
  other arithmetic  44.8 us (23%)
  starting transfers between devices  6.9 us (4%)
  between operations  2.92 us (1%)
    dot_general x12, matrix products, one_head(): jnp.einsum('gtu,ud->tgd', rounded, value_head, preferred_element_type=jnp...  46.1 us
    dot_general x12, matrix products, one_head(): jnp.einsum('tgd,ud->gtu', query_group, key_head, preferred_element_type=j...  32.6 us
    reduce_sum x12, other arithmetic, one_head(): sums = jnp.sum(weights, axis=-1)  24.2 us
    cond x2, local copies, waits for them, and re-layouts, maybe_tile(): return lax.cond(flag, compute, skipped)  20.5 us
    convert_element_type x1, other arithmetic, merge_tiles(): return (weighted / denominator.T[:, :, None]).astype(jnp.bfloat16)  13.7 us
    another operation x4, local copies, waits for them, and re-layouts  13.6 us
    transpose x1, local copies, waits for them, and re-layouts, tile_partial(): outputs.transpose(1, 0, 2, 3).reshape(tile_rows, head_count, head_width)  10.3 us
    unnamed x6, local copies, waits for them, and re-layouts  9.58 us
  transfers between devices with their start and end apart: 2, of which 0 were waited for; matrix products, arithmetic and copies ran while one was open for 57% of the time, Pallas kernels for 0%

commit v1 on v0

v1 whole, which is shorter than its diff:
```python
import functools
import math

import jax
import jax.numpy as jnp
from jax import lax
from jax.experimental import pallas as pl
from jax.experimental.pallas import tpu as pltpu
from jax.sharding import PartitionSpec as P

LANES = 128
BLOCK = 64
STRIPS = 1
MASKED = -1e30
MESH = pl.DeviceIdType.MESH


def kernel(count, lengths, q_hbm, kv_hbm, out_hbm, kbuf, qbuf, obuf, hot, bias, qsem, osem, ksem,
           far_send, far_recv, near_send, near_recv):
    heads, rows, pair = kv_hbm.shape
    width = pair // 2
    group = q_hbm.shape[1] // heads
    span = 2 * rows + LANES
    me = lax.axis_index("ctx")
    odd = lax.rem(me, 2) == 1
    partner = jnp.where(odd, me - 1, me + 1)
    has_up = me + 2 < count
    has_down = me >= 2

    barrier = pltpu.get_barrier_semaphore()

    def greet(other):
        pl.semaphore_signal(barrier, inc=1, device_id={"ctx": other}, device_id_type=MESH)

    def q_copy(h, slot):
        return pltpu.make_async_copy(
            q_hbm.at[:, pl.ds(h * group, group), :], qbuf.at[slot], qsem.at[slot]
        )

    def o_copy(h, slot):
        return pltpu.make_async_copy(
            obuf.at[slot], out_hbm.at[:, pl.ds(h * group, group), :], osem.at[slot]
        )

    def own_copy(h):
        return pltpu.make_async_copy(
            kv_hbm.at[h], kbuf.at[h, pl.ds(2 * rows, rows), :], ksem.at[h]
        )

    def far_copy(h):
        return pltpu.make_async_remote_copy(
            src_ref=kv_hbm.at[h],
            dst_ref=kbuf.at[h, pl.ds(0, rows), :],
            send_sem=far_send.at[h],
            recv_sem=far_recv.at[h],
            device_id={"ctx": me + 2},
            device_id_type=MESH,
        )

    def near_own_copy(h):
        return pltpu.make_async_remote_copy(
            src_ref=kv_hbm.at[h],
            dst_ref=kbuf.at[h, pl.ds(rows, rows), :],
            send_sem=near_send.at[h],
            recv_sem=near_recv.at[h],
            device_id={"ctx": partner},
            device_id_type=MESH,
        )

    def near_relay_copy(h):
        return pltpu.make_async_remote_copy(
            src_ref=kbuf.at[h, pl.ds(0, rows), :],
            dst_ref=kbuf.at[h, pl.ds(rows, rows), :],
            send_sem=near_send.at[h],
            recv_sem=near_recv.at[h],
            device_id={"ctx": partner},
            device_id_type=MESH,
        )

    greet(partner)

    @pl.when(has_up)
    def _():
        greet(me + 2)

    @pl.when(has_down)
    def _():
        greet(me - 2)

    q_copy(0, 0).start()
    for h in range(heads):
        own_copy(h).start()

    pl.semaphore_wait(barrier, 1 + has_up.astype(jnp.int32) + has_down.astype(jnp.int32))

    @pl.when(has_up)
    def _():
        for h in range(heads):
            far_copy(h).start()

    @pl.when(jnp.logical_not(odd))
    def _():
        for h in range(heads):
            near_own_copy(h).start()

    @pl.when(me < 2)
    def _():
        kbuf[:, 0:rows, :] = jnp.zeros((heads, rows, pair), kbuf.dtype)

    @pl.when(me < 1)
    def _():
        kbuf[:, rows : 2 * rows, :] = jnp.zeros((heads, rows, pair), kbuf.dtype)

    row_token = lax.broadcasted_iota(jnp.int32, (BLOCK, group, LANES), 0)
    lane = lax.broadcasted_iota(jnp.int32, (BLOCK, group, LANES), 2)
    hot[...] = (
        jnp.where(row_token == lane, 1.0, 0.0).reshape(BLOCK * group, LANES).astype(hot.dtype)
    )

    def window_of(block):
        return ((block * BLOCK) // LANES) * LANES

    def fill_bias(block, carry):
        base = me * rows
        token = base + block * BLOCK + lax.broadcasted_iota(jnp.int32, (1, LANES), 1)
        first = jnp.zeros((1, LANES), jnp.int32)
        end = jnp.int32(0)
        for d in range(lengths.shape[1]):
            end = end + lengths[0, d]
            first = jnp.where(token >= end, end, first)
        key = base - 2 * rows + window_of(block) + lax.broadcasted_iota(jnp.int32, (span, LANES), 0)
        allowed = (key >= first) & (key <= token)
        bias[block] = jnp.where(allowed, 0.0, MASKED).astype(bias.dtype)
        return carry

    lax.fori_loop(0, rows // BLOCK, fill_bias, 0)

    factor = math.log2(math.e) / math.sqrt(width)
    ones = jnp.ones((span, LANES), kbuf.dtype)

    def one_head(h, carry):
        slot = lax.rem(h, 2)
        q_copy(h, slot).wait()

        @pl.when(h + 1 < heads)
        def _():
            q_copy(h + 1, 1 - slot).start()

        own_copy(h).wait()

        @pl.when(has_down)
        def _():
            far_copy(h).wait_recv()

        @pl.when(has_down & odd)
        def _():
            near_relay_copy(h).start()

        @pl.when(me >= 1)
        def _():
            near_own_copy(h).wait_recv()

        @pl.when(h >= 2)
        def _():
            o_copy(h - 2, slot).wait()

        def one_block(block, inner):
            window = pl.ds(pl.multiple_of(window_of(block), LANES), span)
            both = kbuf[h, window, :]
            keys = jnp.concatenate([both[:, :width], bias[block]], axis=1)
            values = jnp.concatenate([both[:, width:], ones], axis=1)
            tokens = BLOCK // STRIPS
            for s in range(STRIPS):
                at = pl.ds(pl.multiple_of(block * BLOCK, BLOCK) + s * tokens, tokens)
                q = qbuf[slot, at].reshape(tokens * group, width)
                q = jnp.concatenate([q, hot[s * tokens * group : (s + 1) * tokens * group]], axis=1)
                scores = lax.dot_general(
                    q, keys, (((1,), (1,)), ((), ())), preferred_element_type=jnp.float32
                )
                top = jnp.max(scores, axis=1, keepdims=True)
                weights = jnp.exp2((scores - top) * factor).astype(kbuf.dtype)
                total = jnp.dot(weights, values, preferred_element_type=jnp.float32)
                result = total[:, :width] / total[:, width : 2 * width]
                obuf[slot, at] = result.reshape(tokens, group, width).astype(obuf.dtype)
            return inner

        lax.fori_loop(0, rows // BLOCK, one_block, 0)
        o_copy(h, slot).start()
        return carry

    lax.fori_loop(0, heads, one_head, 0)

    for h in range(max(0, heads - 2), heads):
        o_copy(h, h % 2).wait()

    @pl.when(has_up)
    def _():
        for h in range(heads):
            far_copy(h).wait_send()

    @pl.when(jnp.logical_not(odd))
    def _():
        for h in range(heads):
            near_own_copy(h).wait_send()

    @pl.when(has_down & odd)
    def _():
        for h in range(heads):
            near_relay_copy(h).wait_send()


def body(count, queries, keys, values, doc_lengths):
    rows, query_heads, width = queries.shape
    heads = keys.shape[1]
    group = query_heads // heads
    key_value = jnp.concatenate([keys, values], axis=-1).transpose(1, 0, 2)
    blocks = rows // BLOCK
    span = 2 * rows + LANES
    any_space = pl.BlockSpec(memory_space=pl.ANY)
    return pl.pallas_call(
        functools.partial(kernel, count),
        out_shape=jax.ShapeDtypeStruct(queries.shape, queries.dtype),
        in_specs=[pl.BlockSpec(memory_space=pltpu.SMEM), any_space, any_space],
        out_specs=any_space,
        scratch_shapes=[
            pltpu.VMEM((heads, 3 * rows, 2 * width), keys.dtype),
            pltpu.VMEM((2, rows, group, width), queries.dtype),
            pltpu.VMEM((2, rows, group, width), queries.dtype),
            pltpu.VMEM((BLOCK * group, LANES), queries.dtype),
            pltpu.VMEM((blocks, span, LANES), queries.dtype),
            pltpu.SemaphoreType.DMA((2,)),
            pltpu.SemaphoreType.DMA((2,)),
            pltpu.SemaphoreType.DMA((heads,)),
            pltpu.SemaphoreType.DMA((heads,)),
            pltpu.SemaphoreType.DMA((heads,)),
            pltpu.SemaphoreType.DMA((heads,)),
            pltpu.SemaphoreType.DMA((heads,)),
        ],
        compiler_params=pltpu.CompilerParams(
            collective_id=0, has_side_effects=True, vmem_limit_bytes=56 * 1024 * 1024
        ),
    )(doc_lengths, queries, key_value)


def solution(mesh):
    placed = (
        P(("dp", "ctx"), None, None),
        P(("dp", "ctx"), None, None),
        P(("dp", "ctx"), None, None),
        P("dp", None),
    )
    return jax.shard_map(
        functools.partial(body, mesh.shape["ctx"]),
        mesh=mesh,
        in_specs=placed,
        out_specs=P(("dp", "ctx"), None, None),
        check_vma=False,
    )
```

time: 197 us -> 78.1 us (0.40)
  matrix products: 78.8 us -> 0 us
  Pallas kernels: 0 us -> 69.6 us
  local copies, waits for them, and re-layouts: 61.4 us -> 7.14 us
  other arithmetic: 44.8 us -> 1.09 us
  starting transfers between devices: 6.9 us -> 0 us
  between operations: 2.92 us -> 0.02 us
    dot_general x24 -> x0, matrix products: 78.8 us -> none  [the longest x12 46.1 us: one_head(): jnp.einsum('gtu,ud->tgd', rounded, value_head, preferred_element_type=jnp...]
    pallas_call x0 -> x1, Pallas kernels: none -> 69.6 us  [body(): pl.pallas_call(functools.partial(kernel, count), out_shape=jax.ShapeDtype...]
    reduce_sum x16 -> x0, other arithmetic: 24.6 us -> none  [the longest x12 24.2 us: one_head(): sums = jnp.sum(weights, axis=-1)]
    cond x2 -> x0, local copies, waits for them, and re-layouts: 20.5 us -> none  [maybe_tile(): return lax.cond(flag, compute, skipped)]
    convert_element_type x1 -> x0, other arithmetic: 13.7 us -> none  [merge_tiles(): return (weighted / denominator.T[:, :, None]).astype(jnp.bfloat16)]
    another operation x4 -> x0, local copies, waits for them, and re-layouts: 13.6 us -> none
    transpose x9 -> x0, local copies, waits for them, and re-layouts: 12 us -> none  [the longest x1 10.3 us: tile_partial(): outputs.transpose(1, 0, 2, 3).reshape(tile_rows, head_count, head_width)]
    ppermute x2 -> x0, starting transfers between devices: 6.9 us -> none  [shifted(): lax.ppermute(value, axis, [(source, source + steps) for source in range(f...]
  transfers between devices with their start and end apart: 2 -> 0, of which waited for: 0 -> 0; matrix products, arithmetic and copies ran while one was open for 57% -> 0% of each run, Pallas kernels for 0% -> 0%
where the time goes in v1:
time: 78.1 us; the launch traced here: 77.9 us
  Pallas kernels  69.6 us (89%)
  local copies, waits for them, and re-layouts  7.14 us (9%)
  other arithmetic  1.09 us (1%)
    pallas_call x1, Pallas kernels, body(): pl.pallas_call(functools.partial(kernel, count), out_shape=jax.ShapeDtype...  69.6 us
    unnamed x3, local copies, waits for them, and re-layouts  7.14 us

profile of v1, /device:TPU:8, one launch (start us, length us, event | category | flops | bytes accessed | tf_op | source)
XLA Modules:
  0.0 77.9 jit_solution(5508542015924677276)
XLA Ops:
  0.0 1.1 %copy.5 = bf16[512,4,128]{2,0,1:T(8,128)(2,1)S(1)} copy(bf16[512,4,128]{2,1,0:T(4,128)(2,1)} %param.5) | data formatting | bytes 1048576 | tf_op args[1]
  1.1 1.1 %copy.6 = bf16[512,4,128]{2,0,1:T(8,128)(2,1)S(1)} copy(bf16[512,4,128]{2,1,0:T(4,128)(2,1)} %param.6) | data formatting | bytes 1048576 | tf_op args[2]
  2.2 1.1 %maximum_bitcast_fusion.kv_hbm = bf16[4,512,256]{2,1,0:T(8,128)(2,1)} fusion(bf16[512,4,128]{2,0,1:T(8,128)(2,1)S(1)} %copy.6, bf16[512,4,128]{2,0,1:T(8,128)(2,1)S(1)} %copy.5), kind=kLoop, calls=%fused_computation | loop fusion | flops 2097152 | bytes 2097152 | tf_op jit(solution)/shard_map/transpose | solution.py:216
  3.3 69.6 %shard_map.46 = bf16[512,32,128]{2,1,0:T(8,128)(2,1)} custom-call(s32[1,8]{1,0:T(1,128)} %lengths.1, bf16[512,32,128]{2,1,0:T(8,128)(2,1)} %q_hbm.1, bf16[4,512,256]{2,1,0:T(8,128)(2,1)} %maximum_bitcast_fusion.kv_hbm), custom_call_target="tpu_custom_call" | custom-call | tf_op jit(solution)/shard_map/pallas_call | solution.py:220
  73.0 4.9 %copy.8 = bf16[512,32,128]{2,1,0:T(8,128)(2,1)} copy(bf16[512,32,128]{2,1,0:T(8,128)(2,1)} %shard_map.46) | data formatting | bytes 8388608

commit v2 on v1

v2 whole, which is shorter than its diff:
```python
import functools
import math

import jax
import jax.numpy as jnp
from jax import lax
from jax.experimental import pallas as pl
from jax.experimental.pallas import tpu as pltpu
from jax.sharding import PartitionSpec as P

LANES = 128
BLOCK = 64
MASKED = -1e30
MESH = pl.DeviceIdType.MESH


def kernel(count, lengths, q_hbm, k_hbm, v_hbm, out_hbm, kbuf, vbuf, qbuf, obuf, hot, bias, scores_a,
           scores_b, tops_a, tops_b, qsem, osem, ksem, far_send, far_recv, near_send, near_recv):
    heads, rows, width = k_hbm.shape
    parts = ((k_hbm, kbuf), (v_hbm, vbuf))
    group = q_hbm.shape[1] // heads
    span = 2 * rows + LANES
    me = lax.axis_index("ctx")
    odd = lax.rem(me, 2) == 1
    partner = jnp.where(odd, me - 1, me + 1)
    has_up = me + 2 < count
    has_down = me >= 2

    barrier = pltpu.get_barrier_semaphore()

    def greet(other):
        pl.semaphore_signal(barrier, inc=1, device_id={"ctx": other}, device_id_type=MESH)

    def q_copy(h, slot):
        return pltpu.make_async_copy(
            q_hbm.at[:, pl.ds(h * group, group), :], qbuf.at[slot], qsem.at[slot]
        )

    def o_copy(h, slot):
        return pltpu.make_async_copy(
            obuf.at[slot], out_hbm.at[:, pl.ds(h * group, group), :], osem.at[slot]
        )

    def own_copy(h, part):
        source, held = parts[part]
        return pltpu.make_async_copy(
            source.at[h], held.at[h, pl.ds(2 * rows, rows), :], ksem.at[2 * h + part]
        )

    def far_copy(h, part):
        source, held = parts[part]
        return pltpu.make_async_remote_copy(
            src_ref=source.at[h],
            dst_ref=held.at[h, pl.ds(0, rows), :],
            send_sem=far_send.at[2 * h + part],
            recv_sem=far_recv.at[2 * h + part],
            device_id={"ctx": me + 2},
            device_id_type=MESH,
        )

    def near_own_copy(h, part):
        source, held = parts[part]
        return pltpu.make_async_remote_copy(
            src_ref=source.at[h],
            dst_ref=held.at[h, pl.ds(rows, rows), :],
            send_sem=near_send.at[2 * h + part],
            recv_sem=near_recv.at[2 * h + part],
            device_id={"ctx": partner},
            device_id_type=MESH,
        )

    def near_relay_copy(h, part):
        held = parts[part][1]
        return pltpu.make_async_remote_copy(
            src_ref=held.at[h, pl.ds(0, rows), :],
            dst_ref=held.at[h, pl.ds(rows, rows), :],
            send_sem=near_send.at[2 * h + part],
            recv_sem=near_recv.at[2 * h + part],
            device_id={"ctx": partner},
            device_id_type=MESH,
        )

    greet(partner)

    @pl.when(has_up)
    def _():
        greet(me + 2)

    @pl.when(has_down)
    def _():
        greet(me - 2)

    q_copy(0, 0).start()
    for h in range(heads):
        for part in range(2):
            own_copy(h, part).start()

    pl.semaphore_wait(barrier, 1 + has_up.astype(jnp.int32) + has_down.astype(jnp.int32))

    @pl.when(has_up)
    def _():
        for h in range(heads):
            for part in range(2):
                far_copy(h, part).start()

    @pl.when(jnp.logical_not(odd))
    def _():
        for h in range(heads):
            for part in range(2):
                near_own_copy(h, part).start()

    @pl.when(me < 2)
    def _():
        for held in (kbuf, vbuf):
            held[:, 0:rows, :] = jnp.zeros((heads, rows, width), held.dtype)

    @pl.when(me < 1)
    def _():
        for held in (kbuf, vbuf):
            held[:, rows : 2 * rows, :] = jnp.zeros((heads, rows, width), held.dtype)

    row_token = lax.broadcasted_iota(jnp.int32, (BLOCK, group, LANES), 0)
    lane = lax.broadcasted_iota(jnp.int32, (BLOCK, group, LANES), 2)
    hot[...] = (
        jnp.where(row_token == lane, 1.0, 0.0).reshape(BLOCK * group, LANES).astype(hot.dtype)
    )

    def window_of(block):
        return ((block * BLOCK) // LANES) * LANES

    def fill_bias(block, carry):
        base = me * rows
        token = base + block * BLOCK + lax.broadcasted_iota(jnp.int32, (1, LANES), 1)
        first = jnp.zeros((1, LANES), jnp.int32)
        end = jnp.int32(0)
        for d in range(lengths.shape[1]):
            end = end + lengths[0, d]
            first = jnp.where(token >= end, end, first)
        key = base - 2 * rows + window_of(block) + lax.broadcasted_iota(jnp.int32, (span, LANES), 0)
        allowed = (key >= first) & (key <= token)
        bias[block] = jnp.where(allowed, 0.0, MASKED).astype(bias.dtype)
        return carry

    lax.fori_loop(0, rows // BLOCK, fill_bias, 0)

    factor = math.log2(math.e) / math.sqrt(width)
    ones = jnp.ones((span, LANES), kbuf.dtype)

    blocks = rows // BLOCK
    steps = heads * blocks

    def advance(h):
        @pl.when(has_down)
        def _():
            for part in range(2):
                far_copy(h, part).wait_recv()

                @pl.when(odd)
                def _():
                    near_relay_copy(h, part).start()

    def open_head(h):
        q_copy(h, lax.rem(h, 2)).wait()
        for part in range(2):
            own_copy(h, part).wait()

        @pl.when(me >= 1)
        def _():
            for part in range(2):
                near_own_copy(h, part).wait_recv()

    def score_stage(step, scores, tops):
        h, block = step // blocks, lax.rem(step, blocks)
        window = pl.ds(pl.multiple_of(window_of(block), LANES), span)
        keys = jnp.concatenate([kbuf[h, window, :], bias[block]], axis=1)
        at = pl.ds(pl.multiple_of(block * BLOCK, BLOCK), BLOCK)
        q = qbuf[lax.rem(h, 2), at].reshape(BLOCK * group, width)
        q = jnp.concatenate([q, hot[...]], axis=1)
        found = lax.dot_general(
            q, keys, (((1,), (1,)), ((), ())), preferred_element_type=jnp.float32
        )
        scores[...] = found
        tops[...] = jnp.broadcast_to(jnp.max(found, axis=1, keepdims=True), tops.shape)

    def value_stage(step, scores, tops):
        h, block = step // blocks, lax.rem(step, blocks)
        window = pl.ds(pl.multiple_of(window_of(block), LANES), span)
        values = jnp.concatenate([vbuf[h, window, :], ones], axis=1)
        at = pl.ds(pl.multiple_of(block * BLOCK, BLOCK), BLOCK)
        top = jnp.concatenate([tops[...]] * (span // LANES), axis=1)
        weights = jnp.exp2((scores[...] - top) * factor).astype(kbuf.dtype)
        total = jnp.dot(weights, values, preferred_element_type=jnp.float32)
        result = total[:, :width] / total[:, width : 2 * width]
        obuf[lax.rem(h, 2), at] = result.reshape(BLOCK, group, width).astype(obuf.dtype)

    advance(0)
    open_head(0)
    score_stage(0, scores_a, tops_a)

    def two_steps(pair_index, carry):
        step = pair_index * 2
        h, block = step // blocks, lax.rem(step, blocks)

        @pl.when((block == 0) & (h >= 2))
        def _():
            o_copy(h - 2, lax.rem(h, 2)).wait()

        @pl.when((block == 0) & (h + 1 < heads))
        def _():
            q_copy(h + 1, lax.rem(h + 1, 2)).start()

        @pl.when((block == ((blocks // 2) // 2) * 2) & (h + 1 < heads))
        def _():
            advance(h + 1)

        @pl.when((block == blocks - 2) & (h + 1 < heads))
        def _():
            open_head(h + 1)

        score_stage(step + 1, scores_b, tops_b)
        value_stage(step, scores_a, tops_a)
        score_stage(jnp.minimum(step + 2, steps - 1), scores_a, tops_a)
        value_stage(step + 1, scores_b, tops_b)

        @pl.when(block == blocks - 2)
        def _():
            o_copy(h, lax.rem(h, 2)).start()

        return carry

    lax.fori_loop(0, steps // 2, two_steps, 0)

    for h in range(max(0, heads - 2), heads):
        o_copy(h, h % 2).wait()

    @pl.when(has_up)
    def _():
        for h in range(heads):
            for part in range(2):
                far_copy(h, part).wait_send()

    @pl.when(jnp.logical_not(odd))
    def _():
        for h in range(heads):
            for part in range(2):
                near_own_copy(h, part).wait_send()

    @pl.when(has_down & odd)
    def _():
        for h in range(heads):
            for part in range(2):
                near_relay_copy(h, part).wait_send()


def body(count, queries, keys, values, doc_lengths):
    rows, query_heads, width = queries.shape
    heads = keys.shape[1]
    group = query_heads // heads
    blocks = rows // BLOCK
    span = 2 * rows + LANES
    any_space = pl.BlockSpec(memory_space=pl.ANY)
    return pl.pallas_call(
        functools.partial(kernel, count),
        out_shape=jax.ShapeDtypeStruct(queries.shape, queries.dtype),
        in_specs=[pl.BlockSpec(memory_space=pltpu.SMEM), any_space, any_space, any_space],
        out_specs=any_space,
        scratch_shapes=[
            pltpu.VMEM((heads, 3 * rows, width), keys.dtype),
            pltpu.VMEM((heads, 3 * rows, width), keys.dtype),
            pltpu.VMEM((2, rows, group, width), queries.dtype),
            pltpu.VMEM((2, rows, group, width), queries.dtype),
            pltpu.VMEM((BLOCK * group, LANES), queries.dtype),
            pltpu.VMEM((blocks, span, LANES), queries.dtype),
            pltpu.VMEM((BLOCK * group, span), jnp.float32),
            pltpu.VMEM((BLOCK * group, span), jnp.float32),
            pltpu.VMEM((BLOCK * group, LANES), jnp.float32),
            pltpu.VMEM((BLOCK * group, LANES), jnp.float32),
            pltpu.SemaphoreType.DMA((2,)),
            pltpu.SemaphoreType.DMA((2,)),
            pltpu.SemaphoreType.DMA((2 * heads,)),
            pltpu.SemaphoreType.DMA((2 * heads,)),
            pltpu.SemaphoreType.DMA((2 * heads,)),
            pltpu.SemaphoreType.DMA((2 * heads,)),
            pltpu.SemaphoreType.DMA((2 * heads,)),
        ],
        compiler_params=pltpu.CompilerParams(
            collective_id=0, has_side_effects=True, vmem_limit_bytes=56 * 1024 * 1024
        ),
    )(doc_lengths, queries, keys.transpose(1, 0, 2), values.transpose(1, 0, 2))


def solution(mesh):
    placed = (
        P(("dp", "ctx"), None, None),
        P(("dp", "ctx"), None, None),
        P(("dp", "ctx"), None, None),
        P("dp", None),
    )
    return jax.shard_map(
        functools.partial(body, mesh.shape["ctx"]),
        mesh=mesh,
        in_specs=placed,
        out_specs=P(("dp", "ctx"), None, None),
        check_vma=False,
    )
```

time: 78.1 us -> 52.7 us (0.67)
  Pallas kernels: 69.6 us -> 45.3 us
  other arithmetic: 1.09 us -> 0 us
    pallas_call x1, Pallas kernels: 69.6 us -> 45.3 us  [body(): pl.pallas_call(functools.partial(kernel, count), out_shape=jax.ShapeDtype...]
    transpose x0 -> x1, local copies, waits for them, and re-layouts: none -> 2.3 us  [body(): values.transpose(1, 0, 2)]
    unnamed x3 -> x1, local copies, waits for them, and re-layouts: 7.14 us -> 4.92 us
    transpose x1 -> x0, other arithmetic: 1.09 us -> none  [body(): key_value = jnp.concatenate([keys, values], axis=-1).transpose(1, 0, 2)]
where the time goes in v2:
time: 52.7 us; the launch traced here: 52.6 us
  Pallas kernels  45.3 us (86%)
  local copies, waits for them, and re-layouts  7.22 us (14%)
    pallas_call x1, Pallas kernels, body(): pl.pallas_call(functools.partial(kernel, count), out_shape=jax.ShapeDtype...  45.3 us
    unnamed x1, local copies, waits for them, and re-layouts  4.92 us
    transpose x1, local copies, waits for them, and re-layouts, body(): values.transpose(1, 0, 2)  2.3 us

profile of v2, /device:TPU:8, one launch (start us, length us, event | category | flops | bytes accessed | tf_op | source)
XLA Modules:
  0.0 52.6 jit_solution(12596563026029005050)
XLA Ops:
  0.0 2.3 %copy_bitcast_fusion = (bf16[4,512,128]{2,1,0:T(8,128)(2,1)}, bf16[4,512,128]{2,1,0:T(8,128)(2,1)}) fusion(bf16[512,4,128]{2,1,0:T(4,128)(2,1)} %param.6, bf16[512,4,128]{2,1,0:T(4,128)(2,1)} %param.5), kind=kLoop, calls=%fused_computation | loop fusion | bytes 2097152 | tf_op jit(solution)/shard_map/transpose | solution.py:289
  2.3 45.3 %shard_map.46 = bf16[512,32,128]{2,1,0:T(8,128)(2,1)} custom-call(s32[1,8]{1,0:T(1,128)} %lengths.1, bf16[512,32,128]{2,1,0:T(8,128)(2,1)} %q_hbm.1, bf16[4,512,128]{2,1,0:T(8,128)(2,1)} %get-tuple-element.6.k_hbm, bf16[4,512,128]{2,1,0:T(8,128)(2,1)} %get-tuple-element.5.v_hbm), custom_call_target="tpu_custom_call" | custom-call | tf_op jit(solution)/shard_map/pallas_call | solution.py:262
  47.6 4.9 %copy.10 = bf16[512,32,128]{2,1,0:T(8,128)(2,1)} copy(bf16[512,32,128]{2,1,0:T(8,128)(2,1)} %shard_map.46) | data formatting | bytes 8388608
